TPU v7x, 32 devices: a whole 2x2x4 slice. The times are simulated.
32 devices in a mesh: node: 16 (over z, y, core), local: 2 (over x).
Axes of the slice: x: 2, y: 2, z: 4, core: 2. Of those that a mesh axis runs over, the one named last changes fastest.
Arguments:
- activations: bfloat16 [4096, 4096], P(('node', 'local')), may hold values from -6 to 6
- out_grads: bfloat16 [4096, 512], P(('node', 'local')), may hold values from -6 to 6
- master: float32 [4096, 512], P(('node', 'local')), may hold values from -0.15 to 0.15
- first_moment: float32 [4096, 512], P(('node', 'local')), may hold values from -0.6 to 0.6
- second_moment: float32 [4096, 512], P(('node', 'local')), may hold values from 0.01 to 1
Outputs:
- new_weight: bfloat16 [4096, 512], P('node')
- new_first: float32 [4096, 512], P(('node', 'local'))
- new_second: float32 [4096, 512], P(('node', 'local'))
All inputs are finite; a program needn't handle non-finite values.
Results may differ from a plain program's by a relative error of at most 0.009.
Values may be sent and summed in bfloat16 or wider, within the bound.
No kernel may reach another device: no remote copies, remote signals or barrier semaphores. Data moves between devices by JAX's collectives and lax.ppermute only.
A program may use at most 128 MiB of HBM per device.

v0:
```python
import functools

import jax
import jax.numpy as jnp
from jax import lax
from jax.experimental import pallas as pl
from jax.experimental.pallas import tpu as pltpu
from jax.sharding import PartitionSpec as P


BLOCK = 256
LANES = 128
CUT = 4
SMALL = pltpu.CompilerParams(vmem_limit_bytes=16 * 2**20)


def quantize(values):
    blocks = values.reshape(values.shape[:-1] + (values.shape[-1] // BLOCK, BLOCK))
    largest = jnp.max(jnp.abs(blocks), axis=-1)
    scale = (largest + 1e-06) / 127.0
    payload = (blocks / scale[..., None]).astype(jnp.bfloat16)
    return (payload.reshape(values.shape), scale)


def restore_sum(payload, scale, axis):
    blocks = payload.reshape(payload.shape[:-1] + (scale.shape[-1], BLOCK))
    values = blocks.astype(jnp.float32) * scale[..., None]
    values = values.reshape(payload.shape)
    return jnp.sum(values, axis=axis)


def plain(activations, out_grads, master, first_moment, second_moment):
    node_count = lax.axis_size("node")
    local_count = lax.axis_size("local")
    own_rows = master.shape[0]
    col_count = master.shape[1]
    token_count = activations.shape[0]
    bands = activations.reshape(token_count, node_count, local_count, own_rows)
    got_inputs = lax.all_to_all(bands, "local", split_axis=2, concat_axis=0, tiled=True)
    got_outputs = lax.all_gather(out_grads, "local", axis=0, tiled=True)
    got_inputs = got_inputs.reshape(local_count, token_count, node_count * own_rows)
    got_outputs = got_outputs.reshape(local_count, token_count, col_count)
    grads = jnp.einsum("ltr,ltk->lrk", got_inputs, got_outputs, preferred_element_type=jnp.float32)
    payload, scale = quantize(grads)
    first_sum = restore_sum(payload, scale, 0).reshape(node_count, own_rows, col_count)
    second_payload, second_scale = quantize(first_sum)
    node_payload, node_scale = (
        lax.all_to_all(second_payload, "node", split_axis=0, concat_axis=0, tiled=True),
        lax.all_to_all(
            second_scale.astype(jnp.bfloat16), "node", split_axis=0, concat_axis=0, tiled=True
        ).astype(second_scale.dtype),
    )
    total = restore_sum(node_payload, node_scale, 0)
    grad_mean = total / (node_count * local_count)
    new_first = 0.9 * first_moment + 0.1 * grad_mean
    new_second = 0.95 * second_moment + 0.05 * grad_mean * grad_mean
    update = new_first / (1.0 - 0.9**10) / (jnp.sqrt(new_second / (1.0 - 0.95**10)) + 1e-08)
    own_weight = (master - 0.01 * update).astype(jnp.bfloat16)
    new_weight = lax.all_gather(own_weight, "local", axis=0, tiled=True)
    return (new_weight, new_first, new_second)


class Grid:
    def __init__(self, node_count):
        self.outer = node_count // 4
        self.count = 2 * node_count

    @staticmethod
    def fits(node_count, local_count, rows):
        outer = node_count // 4
        return (
            node_count % 4 == 0 and outer >= 4 and outer & (outer - 1) == 0 and local_count == 2
        ) and rows % LANES == 0

    def move(self, device, outer=0, core=0, first=0, second=0):
        mine = (device // 2) % 2
        local = (1 - mine) * first + mine * second
        middle = mine * first + (1 - mine) * second
        return device ^ (outer * 8 + middle * 4 + core * 2 + local)

    def permute(self, value, **flips):
        pairs = [(d, self.move(d, **flips)) for d in range(self.count)]
        return lax.ppermute(value, ("node", "local"), pairs)

    def me(self):
        return lax.axis_index("node") * 2 + lax.axis_index("local")


def in_vmem(value):
    return pltpu.with_memory_space_constraint(value, pltpu.VMEM)


def load_kernel(source, out, sem):
    copy = pltpu.make_async_copy(source, out, sem)
    copy.start()
    copy.wait()


def load(value):
    return pl.pallas_call(
        load_kernel,
        out_shape=pltpu.VMEM(value.shape, value.dtype),
        in_specs=[pl.BlockSpec(memory_space=pltpu.HBM)],
        out_specs=pl.BlockSpec(memory_space=pltpu.VMEM),
        scratch_shapes=[pltpu.SemaphoreType.DMA(())],
        compiler_params=SMALL,
        name="load",
    )(pltpu.with_memory_space_constraint(value, pltpu.HBM))


def take_kernel(grid, wanted, rows, own, partner, *outs):
    me = grid.me()
    tokens = own.shape[0]
    for (first, steps), out in zip(wanted, outs):
        at = 0
        for second, step in ((second, step) for second in range(2) for step in steps):
            block = grid.move(me, outer=step, first=first, second=second)
            columns = pl.ds(pl.multiple_of(block * rows, rows), rows)
            out[pl.ds(0, tokens), pl.ds(at, rows)] = own[:, columns]
            out[pl.ds(tokens, tokens), pl.ds(at, rows)] = partner[:, columns]
            at += rows


def take(grid, wanted, rows, own, partner):
    vmem = pl.BlockSpec(memory_space=pltpu.VMEM)
    return pl.pallas_call(
        functools.partial(take_kernel, grid, wanted, rows),
        out_shape=[
            pltpu.VMEM((2 * own.shape[0], 2 * len(steps) * rows), own.dtype) for _, steps in wanted
        ],
        in_specs=[vmem] * 2,
        out_specs=[vmem] * len(wanted),
        compiler_params=SMALL,
        name="take",
    )(in_vmem(own), in_vmem(partner))


def product(left, right):
    return lax.dot_general(
        left, right, (((0,), (0,)), ((), ())), preferred_element_type=jnp.float32
    )


def sums_kernel(first, *refs):
    lefts, rights, out = refs[:2], refs[2:-1], refs[-1]
    columns = pl.ds(first, out.shape[0])
    tokens = rights[0].shape[0]
    total = None
    for i, right in enumerate(rights):
        part = product(lefts[i // 2][pl.ds(i % 2 * tokens, tokens), columns], right[...])
        total = part if total is None else total + part
    out[...] = total.astype(out.dtype)


def sums(first, size, dtype, lefts, rights):
    vmem = pl.BlockSpec(memory_space=pltpu.VMEM)
    operands = (*lefts, *rights)
    return pl.pallas_call(
        functools.partial(sums_kernel, first),
        out_shape=pltpu.VMEM((size, rights[0].shape[1]), dtype),
        in_specs=[vmem] * len(operands),
        out_specs=vmem,
        compiler_params=SMALL,
        name="sums",
    )(*(in_vmem(v) for v in operands))


def merge_kernel(pieces, kept, got, *outs):
    for (start, size, dtype), out in zip(pieces, outs):
        at = pl.ds(start, size)
        out[...] = (kept[at, :] + got[at, :].astype(jnp.float32)).astype(dtype)


def merge(kept, got, pieces):
    vmem = pl.BlockSpec(memory_space=pltpu.VMEM)
    return pl.pallas_call(
        functools.partial(merge_kernel, pieces),
        out_shape=[pltpu.VMEM((size, kept.shape[1]), dtype) for _, size, dtype in pieces],
        in_specs=[vmem] * 2,
        out_specs=[vmem] * len(pieces),
        compiler_params=SMALL,
        name="merge",
    )(in_vmem(kept), in_vmem(got))


def adam(grad, master, first_moment, second_moment):
    new_first = 0.9 * first_moment + 0.1 * grad
    new_second = 0.95 * second_moment + 0.05 * grad * grad
    update = new_first / (1.0 - 0.9**10) / (jnp.sqrt(new_second / (1.0 - 0.95**10)) + 1e-08)
    return (master - 0.01 * update).astype(jnp.bfloat16), new_first, new_second


def update_kernel(count, cuts, weights, shared, *refs):
    master, first_moment, second_moment = refs[:3]
    common, refs = refs[3 : 3 + shared], refs[3 + shared :]
    outs = refs[-1:] if weights else refs[-2:]
    own = (len(refs) - len(outs)) // len(cuts)
    for i, (start, width) in enumerate(cuts):
        at = pl.ds(start, width)
        total = common[0][:, at]
        for part in common[1:]:
            total += part[:, at].astype(jnp.float32)
        for part in refs[i * own : (i + 1) * own]:
            total += part[...].astype(jnp.float32)
        step = adam(total / count, master[:, at], first_moment[:, at], second_moment[:, at])
        if weights:
            outs[0][...] = step[0]
        else:
            outs[0][:, at] = step[1]
            outs[1][:, at] = step[2]


def update(count, cuts, weights, state, common, parts):
    rows, cols = state[0].shape
    vmem = pl.BlockSpec(memory_space=pltpu.VMEM)
    operands = [*state, *common, *(v for part in parts for v in part)]
    if weights:
        out_shape = [pltpu.VMEM((rows, cuts[0][1]), jnp.bfloat16)]
    else:
        out_shape = [pltpu.VMEM((rows, cols), jnp.float32)] * 2
    return pl.pallas_call(
        functools.partial(update_kernel, count, cuts, weights, len(common)),
        out_shape=out_shape,
        in_specs=[vmem] * len(operands),
        out_specs=[vmem] * len(out_shape),
        compiler_params=SMALL,
        name="adam",
    )(*(in_vmem(v) for v in operands))


def join_kernel(*refs):
    *parts, out, sems = refs
    rows = parts[0].shape[0]
    mine = lax.axis_index("local")
    copies = []
    for i, row in enumerate((mine, 1 - mine)):
        start = 0
        for part in parts[i * len(parts) // 2 : (i + 1) * len(parts) // 2]:
            columns = pl.ds(start, part.shape[1])
            copies.append(
                pltpu.make_async_copy(
                    part, out.at[pl.ds(row * rows, rows), columns], sems.at[len(copies)]
                )
            )
            start += part.shape[1]
    for copy in copies:
        copy.start()
    for copy in copies:
        copy.wait()


def joined(own):
    rows = own[0].shape[0]
    pairs = [(0, 1), (1, 0)]
    other = []
    for part in own:
        other.append(lax.ppermute(part, "local", pairs))
    vmem = pl.BlockSpec(memory_space=pltpu.VMEM)
    operands = (*own, *other)
    return pl.pallas_call(
        join_kernel,
        out_shape=jax.ShapeDtypeStruct((2 * rows, sum(p.shape[1] for p in own)), own[0].dtype),
        in_specs=[vmem] * len(operands),
        out_specs=pl.BlockSpec(memory_space=pl.ANY),
        scratch_shapes=[pltpu.SemaphoreType.DMA((len(operands),))],
        compiler_params=SMALL,
        name="join",
    )(*(in_vmem(v) for v in operands))


def per_device(activations, out_grads, *state):
    node_count, local_count = lax.axis_size("node"), lax.axis_size("local")
    if not Grid.fits(node_count, local_count, state[0].shape[0]):
        return plain(activations, out_grads, *state)
    return step(Grid(node_count), activations, out_grads, *state)


def step(grid, activations, out_grads, *state):
    rows = state[0].shape[0]
    cols = out_grads.shape[1]
    odd, even = tuple(range(3, grid.outer, 2)), tuple(range(2, grid.outer, 2))
    half, full = jnp.bfloat16, jnp.float32

    partner_grads = grid.permute(out_grads, core=1)
    partner = grid.permute(activations, core=1)
    rights = [out_grads, partner_grads]
    rights += [grid.permute(v, first=1) for v in rights]
    plan = {"a": odd, "b": (*even, 1), "c": (0,)}
    own_inputs = load(activations)
    wanted = [(first, steps) for steps in plan.values() for first in range(2)]
    taken = take(grid, wanted, rows, own_inputs, partner)
    lefts = {}
    for i, name in enumerate(plan):
        own, message = taken[2 * i : 2 * i + 2]
        lefts[name] = own, grid.permute(message, first=1)

    def added(name):
        size = rows * len(plan[name])
        operands = lefts[name], rights
        sent = sums(size, size, half, *operands)
        got = grid.permute(sent, second=1)
        kept = sums(0, size, full, *operands)
        return kept, got

    def hop(parts, outer):
        part = sum([p.astype(full) for p in parts[1:]], parts[0])
        return grid.permute(part.astype(half), outer=outer)

    most = cols - cols // CUT
    cuts = ((0, most), (most, cols - most))
    split = len(even) * rows
    passed = hop(added("a"), 1)
    part, total = merge(*added("b"), ((split, rows, half), (0, split, full)))
    near = grid.permute(part, outer=1)
    parts = [
        [
            hop([p[i * rows : (i + 1) * rows, start : start + width] for p in (total, passed)], o)
            for i, o in enumerate(even)
        ]
        for start, width in cuts
    ]
    common = [*added("c"), near]

    weights = []
    for j in range(2):
        weights += update(grid.count, cuts[j : j + 1], True, state, common, parts[j : j + 1])
    new_first, new_second = update(grid.count, cuts, False, state, common, parts)
    new_weight = joined(weights)
    return (new_weight, new_first, new_second)


def solution(mesh):
    spec = P(("node", "local"), None)
    return jax.shard_map(
        per_device,
        mesh=mesh,
        in_specs=(spec,) * 5,
        out_specs=(P("node", None), spec, spec),
        check_vma=False,
    )
```

profile of v0, /device:TPU:0, one launch (start us, length us, event | category | flops | bytes accessed | tf_op | source)
XLA Modules:
  0.0 43.4 jit_solution(5957092303810879873)
XLA Ops:
  0.6 0.6 %collective-permute-start = (bf16[128,4096]{1,0:T(8,128)(2,1)}, bf16[128,4096]{1,0:T(8,128)(2,1)S(1)}, u32[]{:S(2)}, u32[]{:S(2)}) collective-permute-start(bf16[128,4096]{1,0:T(8,128)(2,1)} %source.1), channel_id=1, source_target_pairs={{0,2},{1,3},{2,0},{3,1},{4,6},{5,7},{6,4},{7,5},{8,10},{9,11},{10,... | collective-permute-start | bytes 3145736 | tf_op jit(solution)/shard_map/ppermute | solution.py:83
  1.3 2.9 %collective-permute-start.3 = (bf16[128,512]{1,0:T(8,128)(2,1)}, bf16[128,512]{1,0:T(8,128)(2,1)S(1)}, u32[]{:S(2)}, u32[]{:S(2)}) collective-permute-start(bf16[128,512]{1,0:T(8,128)(2,1)} %refs_2_.14), channel_id=1, source_target_pairs={{0,1},{1,0},{2,6},{3,7},{4,5},{5,4},{6,2},{7,3},{8,9},{9,8},{10,14... | collective-permute-start | bytes 393224 | tf_op jit(solution)/shard_map/ppermute | solution.py:83
  4.2 1.2 %load.1.own = bf16[128,4096]{1,0:T(8,128)(2,1)S(1)} custom-call(bf16[128,4096]{1,0:T(8,128)(2,1)} %source.1), custom_call_target="tpu_custom_call" | custom-call | tf_op jit(solution)/shard_map/load/pallas_call | solution.py:100
  5.4 1.3 %collective-permute-start.4 = (bf16[128,512]{1,0:T(8,128)(2,1)S(1)}, bf16[128,512]{1,0:T(8,128)(2,1)S(1)}, u32[]{:S(2)}, u32[]{:S(2)}) collective-permute-start(bf16[128,512]{1,0:T(8,128)(2,1)S(1)} %collective-permute-done.2.refs_3_), channel_id=1, source_target_pairs={{0,1},{1,0},{2,6},{3,7},{4,5},{5,4},{6,2},{7,3},{8,9},{9,8},{10,14... | collective-permute-start | bytes 393224 | tf_op jit(solution)/shard_map/ppermute | solution.py:83
  7.0 0.9 %collective-permute-start.6 = (bf16[256,512]{1,0:T(8,128)(2,1)S(1)}, bf16[256,512]{1,0:T(8,128)(2,1)S(1)}, u32[]{:S(2)}, u32[]{:S(2)}) collective-permute-start(bf16[256,512]{1,0:T(8,128)(2,1)S(1)} %get-tuple-element.16), channel_id=1, source_target_pairs={{0,1},{1,0},{2,6},{3,7},{4,5},{5,4},{6,2},{7,3},{8,9},{9,8},{10,14... | collective-permute-start | bytes 786440 | tf_op jit(solution)/shard_map/ppermute | solution.py:83
  7.9 1.2 %collective-permute-start.9 = (bf16[256,256]{1,0:T(8,128)(2,1)S(1)}, bf16[256,256]{1,0:T(8,128)(2,1)S(1)}, u32[]{:S(2)}, u32[]{:S(2)}) collective-permute-start(bf16[256,256]{1,0:T(8,128)(2,1)S(1)} %get-tuple-element.20), channel_id=1, source_target_pairs={{0,1},{1,0},{2,6},{3,7},{4,5},{5,4},{6,2},{7,3},{8,9},{9,8},{10,14... | collective-permute-start | bytes 393224 | tf_op jit(solution)/shard_map/ppermute | solution.py:83
  9.1 1.4 %collective-permute-done.4.refs_5_ = bf16[128,512]{1,0:T(8,128)(2,1)S(1)} collective-permute-done((bf16[128,512]{1,0:T(8,128)(2,1)S(1)}, bf16[128,512]{1,0:T(8,128)(2,1)S(1)}, u32[]{:S(2)}, u32[]{:S(2)}) %collective-permute-start.4) | collective-permute-done | bytes 131104 | tf_op jit(solution)/shard_map/ppermute | solution.py:83
  10.5 4.4 %collective-permute-done.9.refs_1_ = bf16[256,256]{1,0:T(8,128)(2,1)S(1)} collective-permute-done((bf16[256,256]{1,0:T(8,128)(2,1)S(1)}, bf16[256,256]{1,0:T(8,128)(2,1)S(1)}, u32[]{:S(2)}, u32[]{:S(2)}) %collective-permute-start.9) | collective-permute-done | bytes 131104 | tf_op jit(solution)/shard_map/ppermute | solution.py:83
  14.8 0.3 sums.11
  15.2 1.6 %collective-permute-start.10 = (bf16[128,512]{1,0:T(8,128)(2,1)S(1)}, bf16[128,512]{1,0:T(8,128)(2,1)S(1)}, u32[]{:S(2)}, u32[]{:S(2)}) collective-permute-start(bf16[128,512]{1,0:T(8,128)(2,1)S(1)} %sums.11), channel_id=1, source_target_pairs={{0,4},{1,5},{2,3},{3,2},{4,0},{5,1},{6,7},{7,6},{8,12},{9,13},{10,... | collective-permute-start | bytes 393224 | tf_op jit(solution)/shard_map/ppermute | solution.py:83
  16.8 1.1 %collective-permute-start.1 = (bf16[256,256]{1,0:T(8,128)(2,1)S(1)}, bf16[256,256]{1,0:T(8,128)(2,1)S(1)}, u32[]{:S(2)}, u32[]{:S(2)}) collective-permute-start(bf16[256,256]{1,0:T(8,128)(2,1)S(1)} %get-tuple-element.14), channel_id=1, source_target_pairs={{0,1},{1,0},{2,6},{3,7},{4,5},{5,4},{6,2},{7,3},{8,9},{9,8},{10,14... | collective-permute-start | bytes 393224 | tf_op jit(solution)/shard_map/ppermute | solution.py:83
  17.8 0.3 sums.10
  18.1 0.4 %sums.9 = bf16[256,512]{1,0:T(8,128)(2,1)S(1)} custom-call(bf16[256,512]{1,0:T(8,128)(2,1)S(1)} %get-tuple-element.15.refs_0_, bf16[256,512]{1,0:T(8,128)(2,1)S(1)} %collective-permute-done.6.refs_1_, bf16[128,512]{1,0:T(8,128)(2,1)S(1)} %copy-done, bf16[128,512]{1,0:T(8,128)(2,1)S(1)} %collective-permute-done.2.refs_3_, ...), custom_call_target="tpu_custom_call" | custom-call | tf_op jit(solution)/shard_map/sums/pallas_call | solution.py:158
  18.6 0.6 %collective-permute-start.7 = (bf16[256,512]{1,0:T(8,128)(2,1)S(1)}, bf16[256,512]{1,0:T(8,128)(2,1)S(1)}, u32[]{:S(2)}, u32[]{:S(2)}) collective-permute-start(bf16[256,512]{1,0:T(8,128)(2,1)S(1)} %sums.9), channel_id=1, source_target_pairs={{0,4},{1,5},{2,3},{3,2},{4,0},{5,1},{6,7},{7,6},{8,12},{9,13},{10,... | collective-permute-start | bytes 786440 | tf_op jit(solution)/shard_map/ppermute | solution.py:83
  19.2 1.7 %collective-permute-done.10 = bf16[128,512]{1,0:T(8,128)(2,1)S(1)} collective-permute-done((bf16[128,512]{1,0:T(8,128)(2,1)S(1)}, bf16[128,512]{1,0:T(8,128)(2,1)S(1)}, u32[]{:S(2)}, u32[]{:S(2)}) %collective-permute-start.10) | collective-permute-done | bytes 131104 | tf_op jit(solution)/shard_map/ppermute | solution.py:83
  20.9 1.6 %collective-permute-start.11 = (bf16[128,512]{1,0:T(8,128)(2,1)S(1)}, bf16[128,512]{1,0:T(8,128)(2,1)S(1)}, u32[]{:S(2)}, u32[]{:S(2)}) collective-permute-start(bf16[128,512]{1,0:T(8,128)(2,1)S(1)} %add_convert_fusion), channel_id=1, source_target_pairs={{0,8},{1,9},{2,10},{3,11},{4,12},{5,13},{6,14},{7,15},{8,0},{9,1},... | collective-permute-start | bytes 393224 | tf_op jit(solution)/shard_map/ppermute | solution.py:83
  22.6 0.6 %collective-permute-done.1.refs_1_ = bf16[256,256]{1,0:T(8,128)(2,1)S(1)} collective-permute-done((bf16[256,256]{1,0:T(8,128)(2,1)S(1)}, bf16[256,256]{1,0:T(8,128)(2,1)S(1)}, u32[]{:S(2)}, u32[]{:S(2)}) %collective-permute-start.1) | collective-permute-done | bytes 131104 | tf_op jit(solution)/shard_map/ppermute | solution.py:83
  23.1 0.3 sums.7
  23.4 0.8 %collective-permute-start.5 = (bf16[128,512]{1,0:T(8,128)(2,1)S(1)}, bf16[128,512]{1,0:T(8,128)(2,1)S(1)}, u32[]{:S(2)}, u32[]{:S(2)}) collective-permute-start(bf16[128,512]{1,0:T(8,128)(2,1)S(1)} %sums.7), channel_id=1, source_target_pairs={{0,4},{1,5},{2,3},{3,2},{4,0},{5,1},{6,7},{7,6},{8,12},{9,13},{10,... | collective-permute-start | bytes 393224 | tf_op jit(solution)/shard_map/ppermute | solution.py:83
  24.3 0.4 %sums.8.kept = f32[256,512]{1,0:T(8,128)S(1)} custom-call(bf16[256,512]{1,0:T(8,128)(2,1)S(1)} %get-tuple-element.15.refs_0_, bf16[256,512]{1,0:T(8,128)(2,1)S(1)} %collective-permute-done.6.refs_1_, bf16[128,512]{1,0:T(8,128)(2,1)S(1)} %copy-done, bf16[128,512]{1,0:T(8,128)(2,1)S(1)} %collective-permute-done.2.refs_3_, ...), custom_call_target="tpu_custom_call" | custom-call | tf_op jit(solution)/shard_map/sums/pallas_call | solution.py:158
  25.1 1.7 %collective-permute-start.8 = (bf16[128,512]{1,0:T(8,128)(2,1)S(1)}, bf16[128,512]{1,0:T(8,128)(2,1)S(1)}, u32[]{:S(2)}, u32[]{:S(2)}) collective-permute-start(bf16[128,512]{1,0:T(8,128)(2,1)S(1)} %get-tuple-element.17), channel_id=1, source_target_pairs={{0,8},{1,9},{2,10},{3,11},{4,12},{5,13},{6,14},{7,15},{8,0},{9,1},... | collective-permute-start | bytes 393224 | tf_op jit(solution)/shard_map/ppermute | solution.py:83
  26.8 2.6 %collective-permute-start.12 = (bf16[128,384]{1,0:T(8,128)(2,1)S(1)}, bf16[128,384]{1,0:T(8,128)(2,1)S(1)}, u32[]{:S(2)}, u32[]{:S(2)}) collective-permute-start(bf16[128,384]{1,0:T(8,128)(2,1)S(1)} %add_convert_fusion.1), channel_id=1, source_target_pairs={{0,16},{1,17},{2,18},{3,19},{4,20},{5,21},{6,22},{7,23},{8,24},{9,... | collective-permute-start | bytes 294920 | tf_op jit(solution)/shard_map/ppermute | solution.py:83
  29.4 0.3 sums.6.refs_3_
  29.8 3.1 %collective-permute-done.12.refs_6_ = bf16[128,384]{1,0:T(8,128)(2,1)S(1)} collective-permute-done((bf16[128,384]{1,0:T(8,128)(2,1)S(1)}, bf16[128,384]{1,0:T(8,128)(2,1)S(1)}, u32[]{:S(2)}, u32[]{:S(2)}) %collective-permute-start.12) | collective-permute-done | bytes 98336 | tf_op jit(solution)/shard_map/ppermute | solution.py:83
  33.1 0.6 %collective-permute-start.14 = (bf16[128,384]{1,0:T(8,128)(2,1)S(1)}, bf16[128,384]{1,0:T(8,128)(2,1)S(1)}, u32[]{:S(2)}, u32[]{:S(2)}) collective-permute-start(bf16[128,384]{1,0:T(8,128)(2,1)S(1)} %adam.3.refs_0_), channel_id=1, source_target_pairs={{0,1},{1,0},{2,3},{3,2},{4,5},{5,4},{6,7},{7,6},{8,9},{9,8},{10,11... | collective-permute-start | bytes 294920 | tf_op jit(solution)/shard_map/ppermute | solution.py:257
  33.7 2.6 %collective-permute-start.13 = (bf16[128,128]{1,0:T(8,128)(2,1)S(1)}, bf16[128,128]{1,0:T(8,128)(2,1)S(1)}, u32[]{:S(2)}, u32[]{:S(2)}) collective-permute-start(bf16[128,128]{1,0:T(8,128)(2,1)S(1)} %add_convert_fusion.2), channel_id=1, source_target_pairs={{0,16},{1,17},{2,18},{3,19},{4,20},{5,21},{6,22},{7,23},{8,24},{9,... | collective-permute-start | bytes 98312 | tf_op jit(solution)/shard_map/ppermute | solution.py:83
  36.3 2.3 %collective-permute-done.13.refs_6_.refs_7_ = bf16[128,128]{1,0:T(8,128)(2,1)S(1)} collective-permute-done((bf16[128,128]{1,0:T(8,128)(2,1)S(1)}, bf16[128,128]{1,0:T(8,128)(2,1)S(1)}, u32[]{:S(2)}, u32[]{:S(2)}) %collective-permute-start.13) | collective-permute-done | bytes 32800 | tf_op jit(solution)/shard_map/ppermute | solution.py:83
  38.6 1.6 %collective-permute-start.15 = (bf16[128,128]{1,0:T(8,128)(2,1)S(1)}, bf16[128,128]{1,0:T(8,128)(2,1)S(1)}, u32[]{:S(2)}, u32[]{:S(2)}) collective-permute-start(bf16[128,128]{1,0:T(8,128)(2,1)S(1)} %adam.4.refs_1_), channel_id=1, source_target_pairs={{0,1},{1,0},{2,3},{3,2},{4,5},{5,4},{6,7},{7,6},{8,9},{9,8},{10,11... | collective-permute-start | bytes 98312 | tf_op jit(solution)/shard_map/ppermute | solution.py:257
  40.4 0.7 %copy.8 = f32[128,512]{1,0:T(8,128)} copy(f32[128,512]{1,0:T(8,128)S(1)} %get-tuple-element.24) | data formatting | bytes 524288
  41.1 0.7 %copy.9 = f32[128,512]{1,0:T(8,128)} copy(f32[128,512]{1,0:T(8,128)S(1)} %get-tuple-element.25) | data formatting | bytes 524288
  41.8 0.9 %collective-permute-done.15.refs_3_ = bf16[128,128]{1,0:T(8,128)(2,1)S(1)} collective-permute-done((bf16[128,128]{1,0:T(8,128)(2,1)S(1)}, bf16[128,128]{1,0:T(8,128)(2,1)S(1)}, u32[]{:S(2)}, u32[]{:S(2)}) %collective-permute-start.15) | collective-permute-done | bytes 32800 | tf_op jit(solution)/shard_map/ppermute | solution.py:257
  42.6 0.7 %join.1 = bf16[256,512]{1,0:T(8,128)(2,1)} custom-call(bf16[128,384]{1,0:T(8,128)(2,1)S(1)} %adam.3.refs_0_, bf16[128,128]{1,0:T(8,128)(2,1)S(1)} %adam.4.refs_1_, bf16[128,384]{1,0:T(8,128)(2,1)S(1)} %collective-permute-done.14.refs_2_, bf16[128,128]{1,0:T(8,128)(2,1)S(1)} %collective-permute-done.15.refs_3_), custom_call_target="tpu_custom_call" | custom-call | tf_op jit(solution)/shard_map/join/pallas_call | solution.py:260
  (26 shorter events, 1.2 us)
Async XLA Ops:
  0.6 6.1 %collective-permute-start = (bf16[128,4096]{1,0:T(8,128)(2,1)}, bf16[128,4096]{1,0:T(8,128)(2,1)S(1)}, u32[]{:S(2)}, u32[]{:S(2)}) collective-permute-start(bf16[128,4096]{1,0:T(8,128)(2,1)} %source.1), channel_id=1, source_target_pairs={{0,2},{1,3},{2,0},{3,1},{4,6},{5,7},{6,4},{7,5},{8,10},{9,11},{10,... | collective-permute-start | bytes 3145736 | tf_op jit(solution)/shard_map/ppermute | solution.py:83
  1.2 4.2 %collective-permute-start.2 = (bf16[128,512]{1,0:T(8,128)(2,1)}, bf16[128,512]{1,0:T(8,128)(2,1)S(1)}, u32[]{:S(2)}, u32[]{:S(2)}) collective-permute-start(bf16[128,512]{1,0:T(8,128)(2,1)} %refs_2_.14), channel_id=1, source_target_pairs={{0,2},{1,3},{2,0},{3,1},{4,6},{5,7},{6,4},{7,5},{8,10},{9,11},{10,... | collective-permute-start | bytes 393224 | tf_op jit(solution)/shard_map/ppermute | solution.py:83
  1.3 7.8 %collective-permute-start.3 = (bf16[128,512]{1,0:T(8,128)(2,1)}, bf16[128,512]{1,0:T(8,128)(2,1)S(1)}, u32[]{:S(2)}, u32[]{:S(2)}) collective-permute-start(bf16[128,512]{1,0:T(8,128)(2,1)} %refs_2_.14), channel_id=1, source_target_pairs={{0,1},{1,0},{2,6},{3,7},{4,5},{5,4},{6,2},{7,3},{8,9},{9,8},{10,14... | collective-permute-start | bytes 393224 | tf_op jit(solution)/shard_map/ppermute | solution.py:83
  5.4 9.4 %copy-start = (bf16[128,512]{1,0:T(8,128)(2,1)S(1)}, bf16[128,512]{1,0:T(8,128)(2,1)}, u32[]{:S(2)}) copy-start(bf16[128,512]{1,0:T(8,128)(2,1)} %refs_2_.14) | copy-start | bytes 393220
  5.4 5.0 %collective-permute-start.4 = (bf16[128,512]{1,0:T(8,128)(2,1)S(1)}, bf16[128,512]{1,0:T(8,128)(2,1)S(1)}, u32[]{:S(2)}, u32[]{:S(2)}) collective-permute-start(bf16[128,512]{1,0:T(8,128)(2,1)S(1)} %collective-permute-done.2.refs_3_), channel_id=1, source_target_pairs={{0,1},{1,0},{2,6},{3,7},{4,5},{5,4},{6,2},{7,3},{8,9},{9,8},{10,14... | collective-permute-start | bytes 393224 | tf_op jit(solution)/shard_map/ppermute | solution.py:83
  7.0 11.1 %collective-permute-start.6 = (bf16[256,512]{1,0:T(8,128)(2,1)S(1)}, bf16[256,512]{1,0:T(8,128)(2,1)S(1)}, u32[]{:S(2)}, u32[]{:S(2)}) collective-permute-start(bf16[256,512]{1,0:T(8,128)(2,1)S(1)} %get-tuple-element.16), channel_id=1, source_target_pairs={{0,1},{1,0},{2,6},{3,7},{4,5},{5,4},{6,2},{7,3},{8,9},{9,8},{10,14... | collective-permute-start | bytes 786440 | tf_op jit(solution)/shard_map/ppermute | solution.py:83
  7.9 7.0 %collective-permute-start.9 = (bf16[256,256]{1,0:T(8,128)(2,1)S(1)}, bf16[256,256]{1,0:T(8,128)(2,1)S(1)}, u32[]{:S(2)}, u32[]{:S(2)}) collective-permute-start(bf16[256,256]{1,0:T(8,128)(2,1)S(1)} %get-tuple-element.20), channel_id=1, source_target_pairs={{0,1},{1,0},{2,6},{3,7},{4,5},{5,4},{6,2},{7,3},{8,9},{9,8},{10,14... | collective-permute-start | bytes 393224 | tf_op jit(solution)/shard_map/ppermute | solution.py:83
  15.2 5.7 %collective-permute-start.10 = (bf16[128,512]{1,0:T(8,128)(2,1)S(1)}, bf16[128,512]{1,0:T(8,128)(2,1)S(1)}, u32[]{:S(2)}, u32[]{:S(2)}) collective-permute-start(bf16[128,512]{1,0:T(8,128)(2,1)S(1)} %sums.11), channel_id=1, source_target_pairs={{0,4},{1,5},{2,3},{3,2},{4,0},{5,1},{6,7},{7,6},{8,12},{9,13},{10,... | collective-permute-start | bytes 393224 | tf_op jit(solution)/shard_map/ppermute | solution.py:83
  16.8 6.4 %collective-permute-start.1 = (bf16[256,256]{1,0:T(8,128)(2,1)S(1)}, bf16[256,256]{1,0:T(8,128)(2,1)S(1)}, u32[]{:S(2)}, u32[]{:S(2)}) collective-permute-start(bf16[256,256]{1,0:T(8,128)(2,1)S(1)} %get-tuple-element.14), channel_id=1, source_target_pairs={{0,1},{1,0},{2,6},{3,7},{4,5},{5,4},{6,2},{7,3},{8,9},{9,8},{10,14... | collective-permute-start | bytes 393224 | tf_op jit(solution)/shard_map/ppermute | solution.py:83
  18.6 6.4 %collective-permute-start.7 = (bf16[256,512]{1,0:T(8,128)(2,1)S(1)}, bf16[256,512]{1,0:T(8,128)(2,1)S(1)}, u32[]{:S(2)}, u32[]{:S(2)}) collective-permute-start(bf16[256,512]{1,0:T(8,128)(2,1)S(1)} %sums.9), channel_id=1, source_target_pairs={{0,4},{1,5},{2,3},{3,2},{4,0},{5,1},{6,7},{7,6},{8,12},{9,13},{10,... | collective-permute-start | bytes 786440 | tf_op jit(solution)/shard_map/ppermute | solution.py:83
  20.9 5.8 %collective-permute-start.11 = (bf16[128,512]{1,0:T(8,128)(2,1)S(1)}, bf16[128,512]{1,0:T(8,128)(2,1)S(1)}, u32[]{:S(2)}, u32[]{:S(2)}) collective-permute-start(bf16[128,512]{1,0:T(8,128)(2,1)S(1)} %add_convert_fusion), channel_id=1, source_target_pairs={{0,8},{1,9},{2,10},{3,11},{4,12},{5,13},{6,14},{7,15},{8,0},{9,1},... | collective-permute-start | bytes 393224 | tf_op jit(solution)/shard_map/ppermute | solution.py:83
  23.4 6.3 %collective-permute-start.5 = (bf16[128,512]{1,0:T(8,128)(2,1)S(1)}, bf16[128,512]{1,0:T(8,128)(2,1)S(1)}, u32[]{:S(2)}, u32[]{:S(2)}) collective-permute-start(bf16[128,512]{1,0:T(8,128)(2,1)S(1)} %sums.7), channel_id=1, source_target_pairs={{0,4},{1,5},{2,3},{3,2},{4,0},{5,1},{6,7},{7,6},{8,12},{9,13},{10,... | collective-permute-start | bytes 393224 | tf_op jit(solution)/shard_map/ppermute | solution.py:83
  25.1 7.8 %collective-permute-start.8 = (bf16[128,512]{1,0:T(8,128)(2,1)S(1)}, bf16[128,512]{1,0:T(8,128)(2,1)S(1)}, u32[]{:S(2)}, u32[]{:S(2)}) collective-permute-start(bf16[128,512]{1,0:T(8,128)(2,1)S(1)} %get-tuple-element.17), channel_id=1, source_target_pairs={{0,8},{1,9},{2,10},{3,11},{4,12},{5,13},{6,14},{7,15},{8,0},{9,1},... | collective-permute-start | bytes 393224 | tf_op jit(solution)/shard_map/ppermute | solution.py:83
  26.8 6.1 %copy-start.1 = (f32[128,512]{1,0:T(8,128)S(1)}, f32[128,512]{1,0:T(8,128)}, u32[]{:S(2)}) copy-start(f32[128,512]{1,0:T(8,128)} %refs_0_.5) | copy-start | bytes 786436
  26.8 6.1 %copy-start.2 = (f32[128,512]{1,0:T(8,128)S(1)}, f32[128,512]{1,0:T(8,128)}, u32[]{:S(2)}) copy-start(f32[128,512]{1,0:T(8,128)} %refs_1_.5) | copy-start | bytes 786436
  26.8 6.1 %copy-start.3 = (f32[128,512]{1,0:T(8,128)S(1)}, f32[128,512]{1,0:T(8,128)}, u32[]{:S(2)}) copy-start(f32[128,512]{1,0:T(8,128)} %refs_2_.17) | copy-start | bytes 786436
  26.8 6.1 %collective-permute-start.12 = (bf16[128,384]{1,0:T(8,128)(2,1)S(1)}, bf16[128,384]{1,0:T(8,128)(2,1)S(1)}, u32[]{:S(2)}, u32[]{:S(2)}) collective-permute-start(bf16[128,384]{1,0:T(8,128)(2,1)S(1)} %add_convert_fusion.1), channel_id=1, source_target_pairs={{0,16},{1,17},{2,18},{3,19},{4,20},{5,21},{6,22},{7,23},{8,24},{9,... | collective-permute-start | bytes 294920 | tf_op jit(solution)/shard_map/ppermute | solution.py:83
  33.1 9.5 %collective-permute-start.14 = (bf16[128,384]{1,0:T(8,128)(2,1)S(1)}, bf16[128,384]{1,0:T(8,128)(2,1)S(1)}, u32[]{:S(2)}, u32[]{:S(2)}) collective-permute-start(bf16[128,384]{1,0:T(8,128)(2,1)S(1)} %adam.3.refs_0_), channel_id=1, source_target_pairs={{0,1},{1,0},{2,3},{3,2},{4,5},{5,4},{6,7},{7,6},{8,9},{9,8},{10,11... | collective-permute-start | bytes 294920 | tf_op jit(solution)/shard_map/ppermute | solution.py:257
  33.7 4.9 %collective-permute-start.13 = (bf16[128,128]{1,0:T(8,128)(2,1)S(1)}, bf16[128,128]{1,0:T(8,128)(2,1)S(1)}, u32[]{:S(2)}, u32[]{:S(2)}) collective-permute-start(bf16[128,128]{1,0:T(8,128)(2,1)S(1)} %add_convert_fusion.2), channel_id=1, source_target_pairs={{0,16},{1,17},{2,18},{3,19},{4,20},{5,21},{6,22},{7,23},{8,24},{9,... | collective-permute-start | bytes 98312 | tf_op jit(solution)/shard_map/ppermute | solution.py:83
  38.6 4.0 %collective-permute-start.15 = (bf16[128,128]{1,0:T(8,128)(2,1)S(1)}, bf16[128,128]{1,0:T(8,128)(2,1)S(1)}, u32[]{:S(2)}, u32[]{:S(2)}) collective-permute-start(bf16[128,128]{1,0:T(8,128)(2,1)S(1)} %adam.4.refs_1_), channel_id=1, source_target_pairs={{0,1},{1,0},{2,3},{3,2},{4,5},{5,4},{6,7},{7,6},{8,9},{9,8},{10,11... | collective-permute-start | bytes 98312 | tf_op jit(solution)/shard_map/ppermute | solution.py:257
where the time goes:
time: 43.5 us; the launch traced here: 43.4 us
  starting transfers between devices  21.7 us (50%)
  waiting for transfers between devices  14.5 us (33%)
  Pallas kernels  4.83 us (11%)
  local copies, waits for them, and re-layouts  1.43 us (3%)
  between operations  0.8 us (2%)
    ppermute x14, starting transfers between devices, permute(): return lax.ppermute(value, ('node', 'local'), pairs)  19.5 us
    ppermute x14, waiting for transfers between devices, permute(): return lax.ppermute(value, ('node', 'local'), pairs)  13.7 us
    ppermute x2, starting transfers between devices, joined(): other.append(lax.ppermute(part, 'local', pairs))  2.16 us
    pallas_call x6, Pallas kernels, sums(): pl.pallas_call(functools.partial(sums_kernel, first), out_shape=pltpu.VME...  2.14 us
    unnamed x10, local copies, waits for them, and re-layouts  1.43 us
    pallas_call x1, Pallas kernels, load(): pl.pallas_call(load_kernel, out_shape=pltpu.VMEM(value.shape, value.dtype...  1.23 us
  transfers between devices with their start and end apart: 16, of which 8 were waited for; matrix products, arithmetic and copies ran while one was open for 3% of the time, Pallas kernels for 9%

commit v1 on v0

--- a/solution.py
+++ b/solution.py
@@ -217,7 +217,7 @@
     if weights:
         out_shape = [pltpu.VMEM((rows, cuts[0][1]), jnp.bfloat16)]
     else:
-        out_shape = [pltpu.VMEM((rows, cols), jnp.float32)] * 2
+        out_shape = [jax.ShapeDtypeStruct((rows, cols), jnp.float32)] * 2
     return pl.pallas_call(
         functools.partial(update_kernel, count, cuts, weights, len(common)),
         out_shape=out_shape,
@@ -228,44 +228,46 @@
     )(*(in_vmem(v) for v in operands))
 
 
-def join_kernel(*refs):
-    *parts, out, sems = refs
-    rows = parts[0].shape[0]
+def place_kernel(places, *refs):
+    parts, out, sems = refs[: len(places)], refs[-2], refs[-1]
     mine = lax.axis_index("local")
     copies = []
-    for i, row in enumerate((mine, 1 - mine)):
-        start = 0
-        for part in parts[i * len(parts) // 2 : (i + 1) * len(parts) // 2]:
-            columns = pl.ds(start, part.shape[1])
-            copies.append(
-                pltpu.make_async_copy(
-                    part, out.at[pl.ds(row * rows, rows), columns], sems.at[len(copies)]
-                )
+    for i, (part, (other, start)) in enumerate(zip(parts, places)):
+        rows, width = part.shape
+        row = (1 - mine if other else mine) * rows
+        copies.append(
+            pltpu.make_async_copy(
+                part, out.at[pl.ds(row, rows), pl.ds(start, width)], sems.at[i]
             )
-            start += part.shape[1]
+        )
     for copy in copies:
         copy.start()
     for copy in copies:
         copy.wait()
 
 
+def place(parts, places, shape, *held):
+    return pl.pallas_call(
+        functools.partial(place_kernel, places),
+        out_shape=jax.ShapeDtypeStruct(shape, parts[0].dtype),
+        in_specs=[pl.BlockSpec(memory_space=pltpu.VMEM)] * len(parts)
+        + [pl.BlockSpec(memory_space=pl.ANY)] * len(held),
+        out_specs=pl.BlockSpec(memory_space=pl.ANY),
+        scratch_shapes=[pltpu.SemaphoreType.DMA((len(parts),))],
+        input_output_aliases={len(parts): 0} if held else {},
+        compiler_params=SMALL,
+        name="join",
+    )(*(in_vmem(v) for v in parts), *held)
+
+
 def joined(own):
-    rows = own[0].shape[0]
-    pairs = [(0, 1), (1, 0)]
+    rows, most = own[0].shape
     other = []
     for part in own:
-        other.append(lax.ppermute(part, "local", pairs))
-    vmem = pl.BlockSpec(memory_space=pltpu.VMEM)
-    operands = (*own, *other)
-    return pl.pallas_call(
-        join_kernel,
-        out_shape=jax.ShapeDtypeStruct((2 * rows, sum(p.shape[1] for p in own)), own[0].dtype),
-        in_specs=[vmem] * len(operands),
-        out_specs=pl.BlockSpec(memory_space=pl.ANY),
-        scratch_shapes=[pltpu.SemaphoreType.DMA((len(operands),))],
-        compiler_params=SMALL,
-        name="join",
-    )(*(in_vmem(v) for v in operands))
+        other.append(lax.ppermute(part, "local", [(0, 1), (1, 0)]))
+    shape = (2 * rows, most + own[1].shape[1])
+    held = place((*own, other[0]), ((False, 0), (False, most), (True, 0)), shape)
+    return place((other[1],), ((True, most),), shape, held)
 
 
 def per_device(activations, out_grads, *state):

time: 43.5 us -> 43.4 us (level)
  local copies, waits for them, and re-layouts: 1.43 us -> 0.03 us
  Pallas kernels: 4.83 us -> 6.22 us
    unnamed x10 -> x8, local copies, waits for them, and re-layouts: 1.43 us -> 0.03 us
    pallas_call x3, Pallas kernels: 0.41 us -> 1.2 us  [update(): pl.pallas_call(functools.partial(update_kernel, count, cuts, weights, len...]
    pallas_call x1 -> x2, Pallas kernels: 0.72 us -> 1.33 us  [place(): pl.pallas_call(functools.partial(place_kernel, places), out_shape=jax.Sha...]
  transfers between devices with their start and end apart: 16 -> 16, of which waited for: 8 -> 8; matrix products, arithmetic and copies ran while one was open for 3% -> 0% of each run, Pallas kernels for 9% -> 12%
where the time goes in v1:
time: 43.4 us; the launch traced here: 43.2 us
  starting transfers between devices  21.7 us (50%)
  waiting for transfers between devices  14.4 us (33%)
  Pallas kernels  6.22 us (14%)
  between operations  0.8 us (2%)
    ppermute x14, starting transfers between devices, permute(): return lax.ppermute(value, ('node', 'local'), pairs)  19.5 us
    ppermute x14, waiting for transfers between devices, permute(): return lax.ppermute(value, ('node', 'local'), pairs)  13.7 us
    ppermute x2, starting transfers between devices, joined(): other.append(lax.ppermute(part, 'local', [(0, 1), (1, 0)]))  2.16 us
    pallas_call x6, Pallas kernels, sums(): pl.pallas_call(functools.partial(sums_kernel, first), out_shape=pltpu.VME...  2.14 us
    pallas_call x2, Pallas kernels, place(): pl.pallas_call(functools.partial(place_kernel, places), out_shape=jax.Sha...  1.33 us
    pallas_call x1, Pallas kernels, load(): pl.pallas_call(load_kernel, out_shape=pltpu.VMEM(value.shape, value.dtype...  1.23 us
    pallas_call x3, Pallas kernels, update(): pl.pallas_call(functools.partial(update_kernel, count, cuts, weights, len...  1.2 us
  transfers between devices with their start and end apart: 16, of which 8 were waited for; matrix products, arithmetic and copies ran while one was open for 0% of the time, Pallas kernels for 12%

profile of v1, /device:TPU:0, one launch (start us, length us, event | category | flops | bytes accessed | tf_op | source)
XLA Modules:
  0.0 43.2 jit_solution(16181529602181160329)
XLA Ops:
  0.6 0.6 %collective-permute-start = (bf16[128,4096]{1,0:T(8,128)(2,1)}, bf16[128,4096]{1,0:T(8,128)(2,1)S(1)}, u32[]{:S(2)}, u32[]{:S(2)}) collective-permute-start(bf16[128,4096]{1,0:T(8,128)(2,1)} %source.1), channel_id=1, source_target_pairs={{0,2},{1,3},{2,0},{3,1},{4,6},{5,7},{6,4},{7,5},{8,10},{9,11},{10,... | collective-permute-start | bytes 3145736 | tf_op jit(solution)/shard_map/ppermute | solution.py:83
  1.3 2.9 %collective-permute-start.3 = (bf16[128,512]{1,0:T(8,128)(2,1)}, bf16[128,512]{1,0:T(8,128)(2,1)S(1)}, u32[]{:S(2)}, u32[]{:S(2)}) collective-permute-start(bf16[128,512]{1,0:T(8,128)(2,1)} %refs_2_.14), channel_id=1, source_target_pairs={{0,1},{1,0},{2,6},{3,7},{4,5},{5,4},{6,2},{7,3},{8,9},{9,8},{10,14... | collective-permute-start | bytes 393224 | tf_op jit(solution)/shard_map/ppermute | solution.py:83
  4.2 1.2 %load.1.own = bf16[128,4096]{1,0:T(8,128)(2,1)S(1)} custom-call(bf16[128,4096]{1,0:T(8,128)(2,1)} %source.1), custom_call_target="tpu_custom_call" | custom-call | tf_op jit(solution)/shard_map/load/pallas_call | solution.py:100
  5.4 1.3 %collective-permute-start.4 = (bf16[128,512]{1,0:T(8,128)(2,1)S(1)}, bf16[128,512]{1,0:T(8,128)(2,1)S(1)}, u32[]{:S(2)}, u32[]{:S(2)}) collective-permute-start(bf16[128,512]{1,0:T(8,128)(2,1)S(1)} %collective-permute-done.2.refs_3_), channel_id=1, source_target_pairs={{0,1},{1,0},{2,6},{3,7},{4,5},{5,4},{6,2},{7,3},{8,9},{9,8},{10,14... | collective-permute-start | bytes 393224 | tf_op jit(solution)/shard_map/ppermute | solution.py:83
  7.0 0.9 %collective-permute-start.6 = (bf16[256,512]{1,0:T(8,128)(2,1)S(1)}, bf16[256,512]{1,0:T(8,128)(2,1)S(1)}, u32[]{:S(2)}, u32[]{:S(2)}) collective-permute-start(bf16[256,512]{1,0:T(8,128)(2,1)S(1)} %get-tuple-element.16), channel_id=1, source_target_pairs={{0,1},{1,0},{2,6},{3,7},{4,5},{5,4},{6,2},{7,3},{8,9},{9,8},{10,14... | collective-permute-start | bytes 786440 | tf_op jit(solution)/shard_map/ppermute | solution.py:83
  7.9 1.2 %collective-permute-start.9 = (bf16[256,256]{1,0:T(8,128)(2,1)S(1)}, bf16[256,256]{1,0:T(8,128)(2,1)S(1)}, u32[]{:S(2)}, u32[]{:S(2)}) collective-permute-start(bf16[256,256]{1,0:T(8,128)(2,1)S(1)} %get-tuple-element.20), channel_id=1, source_target_pairs={{0,1},{1,0},{2,6},{3,7},{4,5},{5,4},{6,2},{7,3},{8,9},{9,8},{10,14... | collective-permute-start | bytes 393224 | tf_op jit(solution)/shard_map/ppermute | solution.py:83
  9.1 1.4 %collective-permute-done.4.refs_5_ = bf16[128,512]{1,0:T(8,128)(2,1)S(1)} collective-permute-done((bf16[128,512]{1,0:T(8,128)(2,1)S(1)}, bf16[128,512]{1,0:T(8,128)(2,1)S(1)}, u32[]{:S(2)}, u32[]{:S(2)}) %collective-permute-start.4) | collective-permute-done | bytes 131104 | tf_op jit(solution)/shard_map/ppermute | solution.py:83
  10.5 4.4 %collective-permute-done.9.refs_1_ = bf16[256,256]{1,0:T(8,128)(2,1)S(1)} collective-permute-done((bf16[256,256]{1,0:T(8,128)(2,1)S(1)}, bf16[256,256]{1,0:T(8,128)(2,1)S(1)}, u32[]{:S(2)}, u32[]{:S(2)}) %collective-permute-start.9) | collective-permute-done | bytes 131104 | tf_op jit(solution)/shard_map/ppermute | solution.py:83
  14.8 0.3 sums.11
  15.2 1.6 %collective-permute-start.10 = (bf16[128,512]{1,0:T(8,128)(2,1)S(1)}, bf16[128,512]{1,0:T(8,128)(2,1)S(1)}, u32[]{:S(2)}, u32[]{:S(2)}) collective-permute-start(bf16[128,512]{1,0:T(8,128)(2,1)S(1)} %sums.11), channel_id=1, source_target_pairs={{0,4},{1,5},{2,3},{3,2},{4,0},{5,1},{6,7},{7,6},{8,12},{9,13},{10,... | collective-permute-start | bytes 393224 | tf_op jit(solution)/shard_map/ppermute | solution.py:83
  16.8 1.1 %collective-permute-start.1 = (bf16[256,256]{1,0:T(8,128)(2,1)S(1)}, bf16[256,256]{1,0:T(8,128)(2,1)S(1)}, u32[]{:S(2)}, u32[]{:S(2)}) collective-permute-start(bf16[256,256]{1,0:T(8,128)(2,1)S(1)} %get-tuple-element.14), channel_id=1, source_target_pairs={{0,1},{1,0},{2,6},{3,7},{4,5},{5,4},{6,2},{7,3},{8,9},{9,8},{10,14... | collective-permute-start | bytes 393224 | tf_op jit(solution)/shard_map/ppermute | solution.py:83
  17.8 0.3 sums.10
  18.1 0.4 %sums.9 = bf16[256,512]{1,0:T(8,128)(2,1)S(1)} custom-call(bf16[256,512]{1,0:T(8,128)(2,1)S(1)} %get-tuple-element.15.refs_0_, bf16[256,512]{1,0:T(8,128)(2,1)S(1)} %collective-permute-done.6.refs_1_, bf16[128,512]{1,0:T(8,128)(2,1)S(1)} %copy-done, bf16[128,512]{1,0:T(8,128)(2,1)S(1)} %collective-permute-done.2.refs_3_, ...), custom_call_target="tpu_custom_call" | custom-call | tf_op jit(solution)/shard_map/sums/pallas_call | solution.py:158
  18.6 0.6 %collective-permute-start.7 = (bf16[256,512]{1,0:T(8,128)(2,1)S(1)}, bf16[256,512]{1,0:T(8,128)(2,1)S(1)}, u32[]{:S(2)}, u32[]{:S(2)}) collective-permute-start(bf16[256,512]{1,0:T(8,128)(2,1)S(1)} %sums.9), channel_id=1, source_target_pairs={{0,4},{1,5},{2,3},{3,2},{4,0},{5,1},{6,7},{7,6},{8,12},{9,13},{10,... | collective-permute-start | bytes 786440 | tf_op jit(solution)/shard_map/ppermute | solution.py:83
  19.2 1.7 %collective-permute-done.10 = bf16[128,512]{1,0:T(8,128)(2,1)S(1)} collective-permute-done((bf16[128,512]{1,0:T(8,128)(2,1)S(1)}, bf16[128,512]{1,0:T(8,128)(2,1)S(1)}, u32[]{:S(2)}, u32[]{:S(2)}) %collective-permute-start.10) | collective-permute-done | bytes 131104 | tf_op jit(solution)/shard_map/ppermute | solution.py:83
  20.9 1.6 %collective-permute-start.11 = (bf16[128,512]{1,0:T(8,128)(2,1)S(1)}, bf16[128,512]{1,0:T(8,128)(2,1)S(1)}, u32[]{:S(2)}, u32[]{:S(2)}) collective-permute-start(bf16[128,512]{1,0:T(8,128)(2,1)S(1)} %add_convert_fusion), channel_id=1, source_target_pairs={{0,8},{1,9},{2,10},{3,11},{4,12},{5,13},{6,14},{7,15},{8,0},{9,1},... | collective-permute-start | bytes 393224 | tf_op jit(solution)/shard_map/ppermute | solution.py:83
  22.6 0.6 %collective-permute-done.1.refs_1_ = bf16[256,256]{1,0:T(8,128)(2,1)S(1)} collective-permute-done((bf16[256,256]{1,0:T(8,128)(2,1)S(1)}, bf16[256,256]{1,0:T(8,128)(2,1)S(1)}, u32[]{:S(2)}, u32[]{:S(2)}) %collective-permute-start.1) | collective-permute-done | bytes 131104 | tf_op jit(solution)/shard_map/ppermute | solution.py:83
  23.1 0.3 sums.7
  23.4 0.8 %collective-permute-start.5 = (bf16[128,512]{1,0:T(8,128)(2,1)S(1)}, bf16[128,512]{1,0:T(8,128)(2,1)S(1)}, u32[]{:S(2)}, u32[]{:S(2)}) collective-permute-start(bf16[128,512]{1,0:T(8,128)(2,1)S(1)} %sums.7), channel_id=1, source_target_pairs={{0,4},{1,5},{2,3},{3,2},{4,0},{5,1},{6,7},{7,6},{8,12},{9,13},{10,... | collective-permute-start | bytes 393224 | tf_op jit(solution)/shard_map/ppermute | solution.py:83
  24.3 0.4 %sums.8.kept = f32[256,512]{1,0:T(8,128)S(1)} custom-call(bf16[256,512]{1,0:T(8,128)(2,1)S(1)} %get-tuple-element.15.refs_0_, bf16[256,512]{1,0:T(8,128)(2,1)S(1)} %collective-permute-done.6.refs_1_, bf16[128,512]{1,0:T(8,128)(2,1)S(1)} %copy-done, bf16[128,512]{1,0:T(8,128)(2,1)S(1)} %collective-permute-done.2.refs_3_, ...), custom_call_target="tpu_custom_call" | custom-call | tf_op jit(solution)/shard_map/sums/pallas_call | solution.py:158
  25.1 1.7 %collective-permute-start.8 = (bf16[128,512]{1,0:T(8,128)(2,1)S(1)}, bf16[128,512]{1,0:T(8,128)(2,1)S(1)}, u32[]{:S(2)}, u32[]{:S(2)}) collective-permute-start(bf16[128,512]{1,0:T(8,128)(2,1)S(1)} %get-tuple-element.17), channel_id=1, source_target_pairs={{0,8},{1,9},{2,10},{3,11},{4,12},{5,13},{6,14},{7,15},{8,0},{9,1},... | collective-permute-start | bytes 393224 | tf_op jit(solution)/shard_map/ppermute | solution.py:83
  26.8 2.6 %collective-permute-start.14 = (bf16[128,384]{1,0:T(8,128)(2,1)S(1)}, bf16[128,384]{1,0:T(8,128)(2,1)S(1)}, u32[]{:S(2)}, u32[]{:S(2)}) collective-permute-start(bf16[128,384]{1,0:T(8,128)(2,1)S(1)} %add_convert_fusion.1), channel_id=1, source_target_pairs={{0,16},{1,17},{2,18},{3,19},{4,20},{5,21},{6,22},{7,23},{8,24},{9,... | collective-permute-start | bytes 294920 | tf_op jit(solution)/shard_map/ppermute | solution.py:83
  29.4 0.3 sums.6.refs_3_
  29.8 3.1 %collective-permute-done.14.refs_6_ = bf16[128,384]{1,0:T(8,128)(2,1)S(1)} collective-permute-done((bf16[128,384]{1,0:T(8,128)(2,1)S(1)}, bf16[128,384]{1,0:T(8,128)(2,1)S(1)}, u32[]{:S(2)}, u32[]{:S(2)}) %collective-permute-start.14) | collective-permute-done | bytes 98336 | tf_op jit(solution)/shard_map/ppermute | solution.py:83
  33.1 0.6 %collective-permute-start.15 = (bf16[128,384]{1,0:T(8,128)(2,1)S(1)}, bf16[128,384]{1,0:T(8,128)(2,1)S(1)}, u32[]{:S(2)}, u32[]{:S(2)}) collective-permute-start(bf16[128,384]{1,0:T(8,128)(2,1)S(1)} %adam.4.refs_0_), channel_id=1, source_target_pairs={{0,1},{1,0},{2,3},{3,2},{4,5},{5,4},{6,7},{7,6},{8,9},{9,8},{10,11... | collective-permute-start | bytes 294920 | tf_op jit(solution)/shard_map/ppermute | solution.py:267
  33.7 2.6 %collective-permute-start.12 = (bf16[128,128]{1,0:T(8,128)(2,1)S(1)}, bf16[128,128]{1,0:T(8,128)(2,1)S(1)}, u32[]{:S(2)}, u32[]{:S(2)}) collective-permute-start(bf16[128,128]{1,0:T(8,128)(2,1)S(1)} %add_convert_fusion.2), channel_id=1, source_target_pairs={{0,16},{1,17},{2,18},{3,19},{4,20},{5,21},{6,22},{7,23},{8,24},{9,... | collective-permute-start | bytes 98312 | tf_op jit(solution)/shard_map/ppermute | solution.py:83
  36.3 2.3 %collective-permute-done.12.refs_6_.refs_7_ = bf16[128,128]{1,0:T(8,128)(2,1)S(1)} collective-permute-done((bf16[128,128]{1,0:T(8,128)(2,1)S(1)}, bf16[128,128]{1,0:T(8,128)(2,1)S(1)}, u32[]{:S(2)}, u32[]{:S(2)}) %collective-permute-start.12) | collective-permute-done | bytes 32800 | tf_op jit(solution)/shard_map/ppermute | solution.py:83
  38.6 1.6 %collective-permute-start.13 = (bf16[128,128]{1,0:T(8,128)(2,1)S(1)}, bf16[128,128]{1,0:T(8,128)(2,1)S(1)}, u32[]{:S(2)}, u32[]{:S(2)}) collective-permute-start(bf16[128,128]{1,0:T(8,128)(2,1)S(1)} %adam.3.refs_1_), channel_id=1, source_target_pairs={{0,1},{1,0},{2,3},{3,2},{4,5},{5,4},{6,7},{7,6},{8,9},{9,8},{10,11... | collective-permute-start | bytes 98312 | tf_op jit(solution)/shard_map/ppermute | solution.py:267
  40.2 0.9 %adam.5 = (f32[128,512]{1,0:T(8,128)}, f32[128,512]{1,0:T(8,128)}) custom-call(f32[128,512]{1,0:T(8,128)S(1)} %copy-done.1, f32[128,512]{1,0:T(8,128)S(1)} %copy-done.2, f32[128,512]{1,0:T(8,128)S(1)} %copy-done.3, f32[128,512]{1,0:T(8,128)S(1)} %sums.6.refs_3_, bf16[128,512]{1,0:T(8,128)(2,1)S(1)} %collective-permute-done.5.refs_4_, ...), custom_call_target="tpu_custom_call" | custom-call | tf_op jit(solution)/shard_map/adam/pallas_call | solution.py:221
  41.1 0.7 %join.2.refs_1_ = bf16[256,512]{1,0:T(8,128)(2,1)} custom-call(bf16[128,384]{1,0:T(8,128)(2,1)S(1)} %adam.4.refs_0_, bf16[128,128]{1,0:T(8,128)(2,1)S(1)} %adam.3.refs_1_, bf16[128,384]{1,0:T(8,128)(2,1)S(1)} %collective-permute-done.15.refs_2_), custom_call_target="tpu_custom_call" | custom-call | tf_op jit(solution)/shard_map/join/pallas_call | solution.py:250
  41.9 0.8 %collective-permute-done.13.refs_0_ = bf16[128,128]{1,0:T(8,128)(2,1)S(1)} collective-permute-done((bf16[128,128]{1,0:T(8,128)(2,1)S(1)}, bf16[128,128]{1,0:T(8,128)(2,1)S(1)}, u32[]{:S(2)}, u32[]{:S(2)}) %collective-permute-start.13) | collective-permute-done | bytes 32800 | tf_op jit(solution)/shard_map/ppermute | solution.py:267
  42.6 0.6 %join.3 = bf16[256,512]{1,0:T(8,128)(2,1)} custom-call(bf16[128,128]{1,0:T(8,128)(2,1)S(1)} %collective-permute-done.13.refs_0_, bf16[256,512]{1,0:T(8,128)(2,1)} %join.2.refs_1_), custom_call_target="tpu_custom_call", output_to_operand_aliasing={{}: (1, {})} | custom-call | tf_op jit(solution)/shard_map/join/pallas_call | solution.py:250
  (25 shorter events, 1.1 us)
Async XLA Ops:
  0.6 6.1 %collective-permute-start = (bf16[128,4096]{1,0:T(8,128)(2,1)}, bf16[128,4096]{1,0:T(8,128)(2,1)S(1)}, u32[]{:S(2)}, u32[]{:S(2)}) collective-permute-start(bf16[128,4096]{1,0:T(8,128)(2,1)} %source.1), channel_id=1, source_target_pairs={{0,2},{1,3},{2,0},{3,1},{4,6},{5,7},{6,4},{7,5},{8,10},{9,11},{10,... | collective-permute-start | bytes 3145736 | tf_op jit(solution)/shard_map/ppermute | solution.py:83
  1.2 4.2 %collective-permute-start.2 = (bf16[128,512]{1,0:T(8,128)(2,1)}, bf16[128,512]{1,0:T(8,128)(2,1)S(1)}, u32[]{:S(2)}, u32[]{:S(2)}) collective-permute-start(bf16[128,512]{1,0:T(8,128)(2,1)} %refs_2_.14), channel_id=1, source_target_pairs={{0,2},{1,3},{2,0},{3,1},{4,6},{5,7},{6,4},{7,5},{8,10},{9,11},{10,... | collective-permute-start | bytes 393224 | tf_op jit(solution)/shard_map/ppermute | solution.py:83
  1.3 7.8 %collective-permute-start.3 = (bf16[128,512]{1,0:T(8,128)(2,1)}, bf16[128,512]{1,0:T(8,128)(2,1)S(1)}, u32[]{:S(2)}, u32[]{:S(2)}) collective-permute-start(bf16[128,512]{1,0:T(8,128)(2,1)} %refs_2_.14), channel_id=1, source_target_pairs={{0,1},{1,0},{2,6},{3,7},{4,5},{5,4},{6,2},{7,3},{8,9},{9,8},{10,14... | collective-permute-start | bytes 393224 | tf_op jit(solution)/shard_map/ppermute | solution.py:83
  5.4 9.4 %copy-start = (bf16[128,512]{1,0:T(8,128)(2,1)S(1)}, bf16[128,512]{1,0:T(8,128)(2,1)}, u32[]{:S(2)}) copy-start(bf16[128,512]{1,0:T(8,128)(2,1)} %refs_2_.14) | copy-start | bytes 393220
  5.4 5.0 %collective-permute-start.4 = (bf16[128,512]{1,0:T(8,128)(2,1)S(1)}, bf16[128,512]{1,0:T(8,128)(2,1)S(1)}, u32[]{:S(2)}, u32[]{:S(2)}) collective-permute-start(bf16[128,512]{1,0:T(8,128)(2,1)S(1)} %collective-permute-done.2.refs_3_), channel_id=1, source_target_pairs={{0,1},{1,0},{2,6},{3,7},{4,5},{5,4},{6,2},{7,3},{8,9},{9,8},{10,14... | collective-permute-start | bytes 393224 | tf_op jit(solution)/shard_map/ppermute | solution.py:83
  7.0 11.1 %collective-permute-start.6 = (bf16[256,512]{1,0:T(8,128)(2,1)S(1)}, bf16[256,512]{1,0:T(8,128)(2,1)S(1)}, u32[]{:S(2)}, u32[]{:S(2)}) collective-permute-start(bf16[256,512]{1,0:T(8,128)(2,1)S(1)} %get-tuple-element.16), channel_id=1, source_target_pairs={{0,1},{1,0},{2,6},{3,7},{4,5},{5,4},{6,2},{7,3},{8,9},{9,8},{10,14... | collective-permute-start | bytes 786440 | tf_op jit(solution)/shard_map/ppermute | solution.py:83
  7.9 7.0 %collective-permute-start.9 = (bf16[256,256]{1,0:T(8,128)(2,1)S(1)}, bf16[256,256]{1,0:T(8,128)(2,1)S(1)}, u32[]{:S(2)}, u32[]{:S(2)}) collective-permute-start(bf16[256,256]{1,0:T(8,128)(2,1)S(1)} %get-tuple-element.20), channel_id=1, source_target_pairs={{0,1},{1,0},{2,6},{3,7},{4,5},{5,4},{6,2},{7,3},{8,9},{9,8},{10,14... | collective-permute-start | bytes 393224 | tf_op jit(solution)/shard_map/ppermute | solution.py:83
  15.2 5.7 %collective-permute-start.10 = (bf16[128,512]{1,0:T(8,128)(2,1)S(1)}, bf16[128,512]{1,0:T(8,128)(2,1)S(1)}, u32[]{:S(2)}, u32[]{:S(2)}) collective-permute-start(bf16[128,512]{1,0:T(8,128)(2,1)S(1)} %sums.11), channel_id=1, source_target_pairs={{0,4},{1,5},{2,3},{3,2},{4,0},{5,1},{6,7},{7,6},{8,12},{9,13},{10,... | collective-permute-start | bytes 393224 | tf_op jit(solution)/shard_map/ppermute | solution.py:83
  16.8 6.4 %collective-permute-start.1 = (bf16[256,256]{1,0:T(8,128)(2,1)S(1)}, bf16[256,256]{1,0:T(8,128)(2,1)S(1)}, u32[]{:S(2)}, u32[]{:S(2)}) collective-permute-start(bf16[256,256]{1,0:T(8,128)(2,1)S(1)} %get-tuple-element.14), channel_id=1, source_target_pairs={{0,1},{1,0},{2,6},{3,7},{4,5},{5,4},{6,2},{7,3},{8,9},{9,8},{10,14... | collective-permute-start | bytes 393224 | tf_op jit(solution)/shard_map/ppermute | solution.py:83
  18.6 6.4 %collective-permute-start.7 = (bf16[256,512]{1,0:T(8,128)(2,1)S(1)}, bf16[256,512]{1,0:T(8,128)(2,1)S(1)}, u32[]{:S(2)}, u32[]{:S(2)}) collective-permute-start(bf16[256,512]{1,0:T(8,128)(2,1)S(1)} %sums.9), channel_id=1, source_target_pairs={{0,4},{1,5},{2,3},{3,2},{4,0},{5,1},{6,7},{7,6},{8,12},{9,13},{10,... | collective-permute-start | bytes 786440 | tf_op jit(solution)/shard_map/ppermute | solution.py:83
  20.9 5.8 %collective-permute-start.11 = (bf16[128,512]{1,0:T(8,128)(2,1)S(1)}, bf16[128,512]{1,0:T(8,128)(2,1)S(1)}, u32[]{:S(2)}, u32[]{:S(2)}) collective-permute-start(bf16[128,512]{1,0:T(8,128)(2,1)S(1)} %add_convert_fusion), channel_id=1, source_target_pairs={{0,8},{1,9},{2,10},{3,11},{4,12},{5,13},{6,14},{7,15},{8,0},{9,1},... | collective-permute-start | bytes 393224 | tf_op jit(solution)/shard_map/ppermute | solution.py:83
  23.4 6.3 %collective-permute-start.5 = (bf16[128,512]{1,0:T(8,128)(2,1)S(1)}, bf16[128,512]{1,0:T(8,128)(2,1)S(1)}, u32[]{:S(2)}, u32[]{:S(2)}) collective-permute-start(bf16[128,512]{1,0:T(8,128)(2,1)S(1)} %sums.7), channel_id=1, source_target_pairs={{0,4},{1,5},{2,3},{3,2},{4,0},{5,1},{6,7},{7,6},{8,12},{9,13},{10,... | collective-permute-start | bytes 393224 | tf_op jit(solution)/shard_map/ppermute | solution.py:83
  25.1 7.8 %collective-permute-start.8 = (bf16[128,512]{1,0:T(8,128)(2,1)S(1)}, bf16[128,512]{1,0:T(8,128)(2,1)S(1)}, u32[]{:S(2)}, u32[]{:S(2)}) collective-permute-start(bf16[128,512]{1,0:T(8,128)(2,1)S(1)} %get-tuple-element.17), channel_id=1, source_target_pairs={{0,8},{1,9},{2,10},{3,11},{4,12},{5,13},{6,14},{7,15},{8,0},{9,1},... | collective-permute-start | bytes 393224 | tf_op jit(solution)/shard_map/ppermute | solution.py:83
  26.8 6.1 %copy-start.1 = (f32[128,512]{1,0:T(8,128)S(1)}, f32[128,512]{1,0:T(8,128)}, u32[]{:S(2)}) copy-start(f32[128,512]{1,0:T(8,128)} %refs_0_.5) | copy-start | bytes 786436
  26.8 6.1 %copy-start.2 = (f32[128,512]{1,0:T(8,128)S(1)}, f32[128,512]{1,0:T(8,128)}, u32[]{:S(2)}) copy-start(f32[128,512]{1,0:T(8,128)} %refs_1_.5) | copy-start | bytes 786436
  26.8 6.1 %copy-start.3 = (f32[128,512]{1,0:T(8,128)S(1)}, f32[128,512]{1,0:T(8,128)}, u32[]{:S(2)}) copy-start(f32[128,512]{1,0:T(8,128)} %refs_2_.17) | copy-start | bytes 786436
  26.8 6.1 %collective-permute-start.14 = (bf16[128,384]{1,0:T(8,128)(2,1)S(1)}, bf16[128,384]{1,0:T(8,128)(2,1)S(1)}, u32[]{:S(2)}, u32[]{:S(2)}) collective-permute-start(bf16[128,384]{1,0:T(8,128)(2,1)S(1)} %add_convert_fusion.1), channel_id=1, source_target_pairs={{0,16},{1,17},{2,18},{3,19},{4,20},{5,21},{6,22},{7,23},{8,24},{9,... | collective-permute-start | bytes 294920 | tf_op jit(solution)/shard_map/ppermute | solution.py:83
  33.1 8.1 %collective-permute-start.15 = (bf16[128,384]{1,0:T(8,128)(2,1)S(1)}, bf16[128,384]{1,0:T(8,128)(2,1)S(1)}, u32[]{:S(2)}, u32[]{:S(2)}) collective-permute-start(bf16[128,384]{1,0:T(8,128)(2,1)S(1)} %adam.4.refs_0_), channel_id=1, source_target_pairs={{0,1},{1,0},{2,3},{3,2},{4,5},{5,4},{6,7},{7,6},{8,9},{9,8},{10,11... | collective-permute-start | bytes 294920 | tf_op jit(solution)/shard_map/ppermute | solution.py:267
  33.7 4.9 %collective-permute-start.12 = (bf16[128,128]{1,0:T(8,128)(2,1)S(1)}, bf16[128,128]{1,0:T(8,128)(2,1)S(1)}, u32[]{:S(2)}, u32[]{:S(2)}) collective-permute-start(bf16[128,128]{1,0:T(8,128)(2,1)S(1)} %add_convert_fusion.2), channel_id=1, source_target_pairs={{0,16},{1,17},{2,18},{3,19},{4,20},{5,21},{6,22},{7,23},{8,24},{9,... | collective-permute-start | bytes 98312 | tf_op jit(solution)/shard_map/ppermute | solution.py:83
  38.6 4.0 %collective-permute-start.13 = (bf16[128,128]{1,0:T(8,128)(2,1)S(1)}, bf16[128,128]{1,0:T(8,128)(2,1)S(1)}, u32[]{:S(2)}, u32[]{:S(2)}) collective-permute-start(bf16[128,128]{1,0:T(8,128)(2,1)S(1)} %adam.3.refs_1_), channel_id=1, source_target_pairs={{0,1},{1,0},{2,3},{3,2},{4,5},{5,4},{6,7},{7,6},{8,9},{9,8},{10,11... | collective-permute-start | bytes 98312 | tf_op jit(solution)/shard_map/ppermute | solution.py:267
